TPU v7x, 512 devices: a whole 4x4x16 slice. The times are simulated.
512 devices in a mesh: band: 16 (over y_hi, x, core), tm: 32 (over y_lo, z).
Axes of the slice: x: 4, y: 4 (y_hi: 2, y_lo: 2; y = y_hi * 2 + y_lo), z: 16, core: 2. Of those that a mesh axis runs over, the one named last changes fastest.
Arguments:
- spectrum: bfloat16 [64, 128, 65536], P(None, 'band', 'tm'), may hold values from -6 to 6
- w_freq: bfloat16 [5, 64, 8], replicated, may hold values from -1 to 1
- b_freq: float32 [64], replicated, may hold values from -3 to 3
- dilation: int32 [64], replicated, may hold values from 1 to 128, as said below
- w_time: float32 [3, 64], replicated, may hold values from -3 to 3
- b_time: float32 [64], replicated, may hold values from -3 to 3
- w_mix: bfloat16 [128, 128], replicated, may hold values from -0.5 to 0.5
- ln_gain: float32 [64], replicated, may hold values from 0.1 to 1.9
- w_up: bfloat16 [64, 256], replicated, may hold values from -0.75 to 0.75
- b_up: float32 [256], replicated, may hold values from -3 to 3
- w_down: bfloat16 [256, 64], replicated, may hold values from -0.375 to 0.375
- b_down: float32 [64], replicated, may hold values from -3 to 3
- epoch_lengths: int32 [32, 8], P('tm'), may hold values from 1 to 1024, 2048 in all within a row
Outputs:
- epoch_mean: float32 [256, 8192], P('tm', 'band')
- epoch_power: float32 [256, 8192], P('tm', 'band')
Inputs may be any that keep to these rules, and one draw needn't show every extreme that they name: One channel has a dilation of exactly 128.
All inputs are finite; a program needn't handle non-finite values.
Results may differ from a plain program's by a relative error of at most 0.0015.
Values may be sent and summed in bfloat16 or wider, within the bound.
A program may use at most 64 MiB of HBM per device.

v0:
```python
import jax
import jax.numpy as jnp
from jax import lax
from jax.sharding import PartitionSpec as P


def padded_2(block, sides, width, periodic):
    for axis, dim in sides:
        count = lax.axis_size(axis)
        forward = [(i, i + 1) for i in range(count - 1)]
        if periodic:
            forward.append((count - 1, 0))
        backward = [(target, source) for source, target in forward]
        low = lax.ppermute(
            lax.slice_in_dim(block, block.shape[dim] - width, None, axis=dim), axis, forward
        )
        high = lax.ppermute(lax.slice_in_dim(block, 0, width, axis=dim), axis, backward)
        block = jnp.concatenate([low, block, high], axis=dim)
    return block


def dilated(ext, dilation, w_time, b_time, pad, length):

    def one(chan, step, taps, shift):
        left = lax.dynamic_slice_in_dim(chan, pad - step, length, 1).astype(jnp.float32)
        middle = chan[:, pad : pad + length].astype(jnp.float32)
        right = lax.dynamic_slice_in_dim(chan, pad + step, length, 1).astype(jnp.float32)
        return taps[0] * left + taps[1] * middle + taps[2] * right + shift

    return jax.vmap(one)(ext, dilation, w_time.T, b_time).astype(jnp.bfloat16)


def bin_filter(padded, w_freq, b_freq, bins):
    channels = w_freq.shape[1]
    group_size = w_freq.shape[2]
    tiled = jnp.tile(w_freq, (1, 1, channels // group_size))
    owner = jnp.arange(channels) // group_size
    keep = owner[:, None] == owner[None, :]
    blocks = jnp.where(keep[None], tiled, jnp.zeros_like(tiled))
    total = jnp.einsum(
        "co,cft->oft", blocks[0], padded[:, 0:bins], preferred_element_type=jnp.float32
    )
    for tap in range(1, w_freq.shape[0]):
        total = total + jnp.einsum(
            "co,cft->oft",
            blocks[tap],
            padded[:, tap : tap + bins],
            preferred_element_type=jnp.float32,
        )
    return jax.nn.gelu(total + b_freq[:, None, None], approximate=True).astype(jnp.bfloat16)


def on_device(
    spectrum,
    w_freq,
    b_freq,
    dilation,
    w_time,
    b_time,
    w_mix,
    ln_gain,
    w_up,
    b_up,
    w_down,
    b_down,
    epoch_lengths,
):
    channels = spectrum.shape[0]
    local_bins = spectrum.shape[1]
    block_frames = spectrum.shape[2]
    bands = lax.axis_size("band")
    piece = block_frames // bands
    all_bins = local_bins * bands
    padded = padded_2(spectrum, (("band", 1),), 2, False)
    spectral = bin_filter(padded, w_freq, b_freq, local_bins)
    swapped = lax.all_to_all(spectral, "band", split_axis=2, concat_axis=1, tiled=True)
    beside_all = padded_2(swapped, (("band", 2),), piece, True)
    outer_parts = jnp.concatenate([beside_all[:, :, 2 * piece :], beside_all[:, :, :piece]], axis=2)
    outer = padded_2(outer_parts, (("tm", 2),), piece, False)
    band_index = lax.axis_index("band")
    left = jnp.where(band_index == 0, outer[:, :, :piece], beside_all[:, :, :piece])
    right = jnp.where(
        band_index == bands - 1, outer[:, :, 3 * piece :], beside_all[:, :, 2 * piece :]
    )
    joined = jnp.concatenate([left, swapped, right], axis=2)
    filtered = dilated(joined, dilation, w_time, b_time, piece, piece)
    row = epoch_lengths[0]
    ends = jnp.cumsum(row)
    starts = ends - row
    frame_ids = lax.axis_index("band") * piece + jnp.arange(piece, dtype=jnp.int32)
    member = (
        (frame_ids[None, :] >= starts[:, None]) & (frame_ids[None, :] < ends[:, None])
    ).astype(jnp.float32)
    epochs_here = row.shape[0]
    bin_block = min(32, all_bins)

    def per_block(block_id):
        rows = lax.dynamic_slice_in_dim(w_mix, block_id * bin_block, bin_block, 0)
        mixed = jnp.einsum("gf,cfp->cgp", rows, filtered, preferred_element_type=jnp.float32)
        mean = jnp.mean(mixed, axis=0)
        var = jnp.mean((mixed - mean) ** 2, axis=0)
        normed = ((mixed - mean) * lax.rsqrt(var + 1e-05) * ln_gain[:, None, None]).astype(
            jnp.bfloat16
        )
        flat = normed.reshape(channels, bin_block * piece)
        hidden = (
            jnp.einsum("ch,cn->hn", w_up, flat, preferred_element_type=jnp.float32) + b_up[:, None]
        )
        hidden = jax.nn.gelu(hidden, approximate=True).astype(jnp.bfloat16)
        projected = (
            jnp.einsum("hc,hn->cn", w_down, hidden, preferred_element_type=jnp.float32)
            + b_down[:, None]
        )
        resid = lax.dynamic_slice_in_dim(filtered, block_id * bin_block, bin_block, 1).astype(
            jnp.float32
        )
        block_out = projected.reshape(channels, bin_block, piece) + resid
        sums = jnp.einsum("et,cft->efc", member, block_out, precision=lax.Precision.HIGHEST)
        squares = jnp.einsum(
            "et,cft->efc", member, block_out * block_out, precision=lax.Precision.HIGHEST
        )
        return (sums, squares)

    sums, squares = lax.map(per_block, jnp.arange(all_bins // bin_block, dtype=jnp.int32))
    sums = jnp.transpose(sums, (1, 0, 2, 3)).reshape(epochs_here, all_bins * channels)
    squares = jnp.transpose(squares, (1, 0, 2, 3)).reshape(epochs_here, all_bins * channels)
    total_sums, total_squares = (
        lax.psum_scatter(sums, "band", scatter_dimension=1, tiled=True),
        lax.psum_scatter(squares, "band", scatter_dimension=1, tiled=True),
    )
    lens = row.astype(jnp.float32)[:, None]
    return (total_sums / lens, total_squares / lens)


def solution(mesh):
    return jax.shard_map(
        on_device,
        mesh=mesh,
        in_specs=(
            P(None, "band", "tm"),
            P(),
            P(),
            P(),
            P(),
            P(),
            P(),
            P(),
            P(),
            P(),
            P(),
            P(),
            P("tm", None),
        ),
        out_specs=(P("tm", "band"), P("tm", "band")),
        check_vma=False,
    )
```

profile of v0, /device:TPU:2, one launch (start us, length us, event | category | flops | bytes accessed | tf_op | source)
XLA Modules:
  0.0 470.4 jit_solution(17832737130556438430)
XLA Ops:
  7.2 3.3 fusion.61
  10.7 1.9 collective-permute-start
  12.8 3.6 collective-permute-start.1
  16.6 2.8 fusion.54
  19.4 1.8 collective-permute-done
  21.2 1.2 constant_dynamic-update-slice_fusion
  22.5 0.7 fusion.50
  23.2 0.7 fusion.52
  23.9 0.7 fusion.48
  24.6 2.6 fusion.43
  27.3 4.3 copy.55
  31.6 6.3 %reshape.163 = bf16[16,2,32768]{2,1,0:T(2,128)(2,1)S(1)} reshape(bf16[2048,8,64]{2,1,0:T(8,128)(2,1)} %bitcast.139) | data formatting | bytes 4194304
  37.9 35.8 %all_to_all.18 = bf16[16,2,32768]{2,1,0:T(2,128)(2,1)} all-to-all(bf16[16,2,32768]{2,1,0:T(2,128)(2,1)S(1)} %reshape.163), channel_id=1, replica_groups=mesh['band'=16,'tm'=32] {'band'}, dimensions={0} | all-to-all | bytes 4194304 | tf_op jit(solution)/shard_map/all_to_all | solution.py:76
  73.7 7.4 %reshape.164 = bf16[2048,8,64]{2,1,0:T(8,128)(2,1)} reshape(bf16[16,2,32768]{2,1,0:T(2,128)(2,1)} %all_to_all.18) | data formatting | bytes 4194304
  81.1 6.9 %copy.57 = bf16[64,16,8,128]{3,2,1,0:T(8,128)(2,1)} copy(bf16[64,16,8,128]{0,2,3,1:T(8,128)(2,1)} %bitcast.140) | data formatting | bytes 4194304 | tf_op jit(solution)/shard_map/all_to_all | solution.py:76
  88.0 3.3 copy.58
  91.3 2.9 collective-permute-start.2
  94.2 3.4 collective-permute-start.4
  97.6 21.9 %collective-permute-done.2 = bf16[64,128,128]{1,0,2:T(8,128)(2,1)} collective-permute-done((bf16[64,128,128]{1,0,2:T(8,128)(2,1)S(1)}, bf16[64,128,128]{1,0,2:T(8,128)(2,1)}, u32[]{:S(2)}, u32[]{:S(2)}) %collective-permute-start.2) | collective-permute-done | bytes 2097184 | tf_op jit(solution)/shard_map/ppermute | solution.py:14
  119.5 5.3 %collective-permute-start.3 = (bf16[64,128,128]{1,0,2:T(8,128)(2,1)}, bf16[64,128,128]{1,0,2:T(8,128)(2,1)}, u32[]{:S(2)}, u32[]{:S(2)}) collective-permute-start(bf16[64,128,128]{1,0,2:T(8,128)(2,1)} %collective-permute-done.2), channel_id=1, source_target_pairs={{0,1},{1,2},{2,3},{3,4},{4,5},{5,6},{6,7},{7,8},{8,9},{9,10},{10,1... | collective-permute-start | bytes 6291464 | tf_op jit(solution)/shard_map/ppermute | solution.py:14
  124.9 1.3 collective-permute-start.5
  126.4 40.6 %collective-permute-done.3 = bf16[64,128,128]{1,0,2:T(8,128)(2,1)} collective-permute-done((bf16[64,128,128]{1,0,2:T(8,128)(2,1)}, bf16[64,128,128]{1,0,2:T(8,128)(2,1)}, u32[]{:S(2)}, u32[]{:S(2)}) %collective-permute-start.3) | collective-permute-done | bytes 2097184 | tf_op jit(solution)/shard_map/ppermute | solution.py:14
  167.0 1.8 broadcast_select_fusion.1
  168.9 3.6 collective-permute-done.5
  172.5 1.8 broadcast_select_fusion
  174.3 5.7 %pad_maximum_fusion = bf16[64,128,384]{1,0,2:T(8,128)(2,1)} fusion(bf16[64,128,128]{1,0,2:T(8,128)(2,1)S(1)} %broadcast_select_fusion, bf16[64,128,128]{1,0,2:T(8,128)(2,1)S(1)} %copy.58, bf16[64,128,128]{1,0,2:T(8,128)(2,1)S(1)} %broadcast_select_fusion.1), kind=kLoop, calls=%fused_computation.47 | loop fusion | flops 6291456 | bytes 12582912 | tf_op jit(solution)/shard_map/concatenate | solution.py:85
  180.0 9.8 %gather_fusion = bf16[64,128,128]{1,0,2:T(8,128)(2,1)} fusion(bf16[64,128,384]{1,0,2:T(8,128)(2,1)} %pad_maximum_fusion, s32[64]{0:T(128)S(1)} %get-tuple-element.195), kind=kCustom, calls=%fused_computation | custom fusion | bytes 4195072 | tf_op jit(solution)/shard_map/vmap()/gather | solution.py:25
  189.8 9.8 %gather_fusion.1 = bf16[64,128,128]{1,0,2:T(8,128)(2,1)} fusion(bf16[64,128,384]{1,0,2:T(8,128)(2,1)} %pad_maximum_fusion, s32[64]{0:T(128)S(1)} %get-tuple-element.196), kind=kCustom, calls=%fused_computation.1 | custom fusion | bytes 4195072 | tf_op jit(solution)/shard_map/vmap()/gather | solution.py:27
  199.6 5.2 %add_convert_fusion = bf16[64,128,128]{1,0,2:T(8,128)(2,1)} fusion(bf16[64,128,128]{1,0,2:T(8,128)(2,1)} %gather_fusion.1, bf16[64,128,128]{1,0,2:T(8,128)(2,1)S(1)} %copy.58, bf16[64,128,128]{1,0,2:T(8,128)(2,1)} %gather_fusion, f32[64]{0:T(128)S(1)} %copy-done.5, f32[64]{0:T(128)S(1)} %get-tuple-element.191, f32[64]{0:T(128)S(1)} %get-tuple-element.192, ...), kind=kLoop, calls=%fused_computation.57 | loop fusion | flops 10485760 | bytes 8389632 | tf_op jit(solution)/shard_map/convert_element_type | solution.py:30
  204.8 3.4 copy.62
  208.2 67.5 %while.13 = (s32[]{:T(128)}, f32[4,8,32,64]{2,1,3,0:T(8,128)}, f32[4,8,32,64]{2,1,3,0:T(8,128)}, s32[4]{0:T(128)S(1)}, bf16[128,128]{1,0:T(8,128)(2,1)}, /*index...) while((s32[]{:T(128)}, f32[4,8,32,64]{2,1,3,0:T(8,128)}, ...), condition=%wide.region_4.5_spmd.clone, body=%wide.region_1.4_spmd.clone.sunk | while | flops 399519744 | bytes 14905191 | solution.py:124
  208.5 0.6 dynamic_slice.25
  209.7 1.1 fusion.86
  211.0 1.0 multiply_convert_fusion.2
  212.0 3.1 fusion.87
  215.5 4.9 %fusion.89 = f32[4,8,32,64]{2,1,3,0:T(8,128)} fusion(f32[4,8,32,64]{2,1,3,0:T(8,128)} %get-tuple-element.306, s32[]{:T(128)} %get-tuple-element.304, f32[64,32,128]{2,1,0:T(8,128)S(1)} %bitcast_add_fusion.2, s32[128]{0:T(128)S(1)} %get-tuple-element.335, s32[8]{0:T(128)S(1)} %get-tuple-element.334, s32[8]{0:T(128)S(1)} %get-tuple-element.333), kind=kOutput, calls=%fused_computation.18.clone.1 | convolution fusion | flops 25432064 | bytes 1311808 | tf_op jit(solution)/shard_map/while/body/eval_jaxpr/et,cft->efc/dot_general | solution.py:119
  220.4 4.9 %fusion.88 = f32[4,8,32,64]{2,1,3,0:T(8,128)} fusion(f32[4,8,32,64]{2,1,3,0:T(8,128)} %get-tuple-element.305, s32[]{:T(128)} %get-tuple-element.304, f32[64,32,128]{2,1,0:T(8,128)S(1)} %bitcast_add_fusion.2, s32[128]{0:T(128)S(1)} %get-tuple-element.335, s32[8]{0:T(128)S(1)} %get-tuple-element.334, s32[8]{0:T(128)S(1)} %get-tuple-element.333), kind=kOutput, calls=%fused_computation.20.clone.1 | convolution fusion | flops 25169920 | bytes 1311808 | tf_op jit(solution)/shard_map/while/body/eval_jaxpr/et,cft->efc/dot_general | solution.py:118
  225.3 0.6 dynamic_slice.25
  226.5 1.1 fusion.86
  227.8 1.0 multiply_convert_fusion.2
  228.8 3.1 fusion.87
  232.3 4.9 %fusion.89 = f32[4,8,32,64]{2,1,3,0:T(8,128)} fusion(f32[4,8,32,64]{2,1,3,0:T(8,128)} %get-tuple-element.306, s32[]{:T(128)} %get-tuple-element.304, f32[64,32,128]{2,1,0:T(8,128)S(1)} %bitcast_add_fusion.2, s32[128]{0:T(128)S(1)} %get-tuple-element.335, s32[8]{0:T(128)S(1)} %get-tuple-element.334, s32[8]{0:T(128)S(1)} %get-tuple-element.333), kind=kOutput, calls=%fused_computation.18.clone.1 | convolution fusion | flops 25432064 | bytes 1311808 | tf_op jit(solution)/shard_map/while/body/eval_jaxpr/et,cft->efc/dot_general | solution.py:119
  237.2 4.9 %fusion.88 = f32[4,8,32,64]{2,1,3,0:T(8,128)} fusion(f32[4,8,32,64]{2,1,3,0:T(8,128)} %get-tuple-element.305, s32[]{:T(128)} %get-tuple-element.304, f32[64,32,128]{2,1,0:T(8,128)S(1)} %bitcast_add_fusion.2, s32[128]{0:T(128)S(1)} %get-tuple-element.335, s32[8]{0:T(128)S(1)} %get-tuple-element.334, s32[8]{0:T(128)S(1)} %get-tuple-element.333), kind=kOutput, calls=%fused_computation.20.clone.1 | convolution fusion | flops 25169920 | bytes 1311808 | tf_op jit(solution)/shard_map/while/body/eval_jaxpr/et,cft->efc/dot_general | solution.py:118
  242.1 0.6 dynamic_slice.25
  243.3 1.1 fusion.86
  244.7 1.0 multiply_convert_fusion.2
  245.6 3.1 fusion.87
  248.7 0.2 copy.83
  248.9 0.2 bitcast_add_fusion.2
  249.1 4.9 %fusion.89 = f32[4,8,32,64]{2,1,3,0:T(8,128)} fusion(f32[4,8,32,64]{2,1,3,0:T(8,128)} %get-tuple-element.306, s32[]{:T(128)} %get-tuple-element.304, f32[64,32,128]{2,1,0:T(8,128)S(1)} %bitcast_add_fusion.2, s32[128]{0:T(128)S(1)} %get-tuple-element.335, s32[8]{0:T(128)S(1)} %get-tuple-element.334, s32[8]{0:T(128)S(1)} %get-tuple-element.333), kind=kOutput, calls=%fused_computation.18.clone.1 | convolution fusion | flops 25432064 | bytes 1311808 | tf_op jit(solution)/shard_map/while/body/eval_jaxpr/et,cft->efc/dot_general | solution.py:119
  254.0 4.9 %fusion.88 = f32[4,8,32,64]{2,1,3,0:T(8,128)} fusion(f32[4,8,32,64]{2,1,3,0:T(8,128)} %get-tuple-element.305, s32[]{:T(128)} %get-tuple-element.304, f32[64,32,128]{2,1,0:T(8,128)S(1)} %bitcast_add_fusion.2, s32[128]{0:T(128)S(1)} %get-tuple-element.335, s32[8]{0:T(128)S(1)} %get-tuple-element.334, s32[8]{0:T(128)S(1)} %get-tuple-element.333), kind=kOutput, calls=%fused_computation.20.clone.1 | convolution fusion | flops 25169920 | bytes 1311808 | tf_op jit(solution)/shard_map/while/body/eval_jaxpr/et,cft->efc/dot_general | solution.py:118
  258.9 0.6 dynamic_slice.25
  260.2 1.1 fusion.86
  261.5 1.0 multiply_convert_fusion.2
  262.4 3.1 fusion.87
  265.9 4.9 %fusion.89 = f32[4,8,32,64]{2,1,3,0:T(8,128)} fusion(f32[4,8,32,64]{2,1,3,0:T(8,128)} %get-tuple-element.306, s32[]{:T(128)} %get-tuple-element.304, f32[64,32,128]{2,1,0:T(8,128)S(1)} %bitcast_add_fusion.2, s32[128]{0:T(128)S(1)} %get-tuple-element.335, s32[8]{0:T(128)S(1)} %get-tuple-element.334, s32[8]{0:T(128)S(1)} %get-tuple-element.333), kind=kOutput, calls=%fused_computation.18.clone.1 | convolution fusion | flops 25432064 | bytes 1311808 | tf_op jit(solution)/shard_map/while/body/eval_jaxpr/et,cft->efc/dot_general | solution.py:119
  270.8 4.9 %fusion.88 = f32[4,8,32,64]{2,1,3,0:T(8,128)} fusion(f32[4,8,32,64]{2,1,3,0:T(8,128)} %get-tuple-element.305, s32[]{:T(128)} %get-tuple-element.304, f32[64,32,128]{2,1,0:T(8,128)S(1)} %bitcast_add_fusion.2, s32[128]{0:T(128)S(1)} %get-tuple-element.335, s32[8]{0:T(128)S(1)} %get-tuple-element.334, s32[8]{0:T(128)S(1)} %get-tuple-element.333), kind=kOutput, calls=%fused_computation.20.clone.1 | convolution fusion | flops 25169920 | bytes 1311808 | tf_op jit(solution)/shard_map/while/body/eval_jaxpr/et,cft->efc/dot_general | solution.py:118
  275.7 1.5 copy.63
  277.3 0.9 reshape.130
  278.2 1.5 copy.64
  279.8 0.9 reshape.131
  280.7 89.1 %reduce-scatter.3.cloned.1.call-done = f32[8,512]{1,0:T(8,128)} async-done(((f32[8,8192]{1,0:T(8,128)}), f32[8,512]{1,0:T(8,128)}) %reduce-scatter.3.cloned.1.call-update) | async-done | bytes 16400 | tf_op jit(solution)/shard_map/reduce_scatter | solution.py:128
  369.8 92.3 %reduce-scatter.5.cloned.1.call-done = f32[8,512]{1,0:T(8,128)} async-done(((f32[8,8192]{1,0:T(8,128)}), f32[8,512]{1,0:T(8,128)}) %reduce-scatter.5.cloned.1.call-update) | async-done | bytes 16400 | tf_op jit(solution)/shard_map/reduce_scatter | solution.py:129
  462.2 1.4 broadcast_divide_fusion
  (64 shorter events, 2.7 us)
Async XLA Ops:
  7.2 9.4 %copy-start = (bf16[64,8,2048]{2,1,0:T(8,128)(2,1)S(1)}, bf16[64,8,2048]{2,1,0:T(8,128)(2,1)}, u32[]{:S(2)}) copy-start(bf16[64,8,2048]{2,1,0:T(8,128)(2,1)} %param.15) | copy-start | bytes 6291460
  7.2 9.4 %copy-start.2 = (bf16[5,64,8]{1,2,0:T(8,128)(2,1)S(1)}, bf16[5,64,8]{1,2,0:T(8,128)(2,1)}, u32[]{:S(2)}) copy-start(bf16[5,64,8]{1,2,0:T(8,128)(2,1)} %param.16) | copy-start | bytes 15364
  7.2 362.6 %reduce-scatter.3.cloned.1.call-start = ((), (), s32[]{:S(2)}) async-start(), calls=%async_computation.3 | async-start | bytes 278528 | tf_op jit(solution)/shard_map/reduce_scatter | solution.py:128
  10.7 10.5 %collective-permute-start = (bf16[64,2,2048]{2,0,1:T(8,128)(2,1)S(1)}, bf16[64,2,2048]{2,0,1:T(8,128)(2,1)S(1)}, u32[]{:S(2)}, u32[]{:S(2)}) collective-permute-start(bf16[64,2,2048]{2,0,1:T(8,128)(2,1)S(1)} %copy.79), channel_id=1, source_target_pairs={{0,32},{32,64},{64,96},{96,128},{128,160},{160,192},{192,224},{224... | collective-permute-start | bytes 1572872 | tf_op jit(solution)/shard_map/ppermute | solution.py:14
  12.8 11.1 %collective-permute-start.1 = (bf16[64,2,2048]{2,0,1:T(8,128)(2,1)S(1)}, bf16[64,2,2048]{2,0,1:T(8,128)(2,1)S(1)}, u32[]{:S(2)}, u32[]{:S(2)}) collective-permute-start(bf16[64,2,2048]{2,0,1:T(8,128)(2,1)S(1)} %copy.78), channel_id=1, source_target_pairs={{32,0},{64,32},{96,64},{128,96},{160,128},{192,160},{224,192},{256... | collective-permute-start | bytes 1572872 | tf_op jit(solution)/shard_map/ppermute | solution.py:17
  23.9 0.7 copy-start.4
  88.0 38.2 %copy-start.11 = (s32[1,8]{1,0:T(1,128)S(1)}, s32[1,8]{1,0:T(1,128)}, u32[]{:S(2)}) copy-start(s32[1,8]{1,0:T(1,128)} %param.27) | copy-start | bytes 100
  88.0 38.4 %copy-start.9 = (s32[64]{0:T(128)S(1)}, s32[64]{0:T(128)}, u32[]{:S(2)}) copy-start(s32[64]{0:T(128)} %param.18) | copy-start | bytes 772
  88.0 38.4 %copy-start.3 = (f32[3,64]{1,0:T(4,128)S(1)}, f32[3,64]{1,0:T(4,128)}, u32[]{:S(2)}) copy-start(f32[3,64]{1,0:T(4,128)} %param.19) | copy-start | bytes 2308
  91.3 28.2 %collective-permute-start.2 = (bf16[64,128,128]{1,0,2:T(8,128)(2,1)S(1)}, bf16[64,128,128]{1,0,2:T(8,128)(2,1)}, u32[]{:S(2)}, u32[]{:S(2)}) collective-permute-start(bf16[64,128,128]{1,0,2:T(8,128)(2,1)S(1)} %copy.58), channel_id=1, source_target_pairs={{0,32},{32,64},{64,96},{96,128},{128,160},{160,192},{192,224},{224... | collective-permute-start | bytes 6291464 | tf_op jit(solution)/shard_map/ppermute | solution.py:14
  94.2 30.6 %collective-permute-start.4 = (bf16[64,128,128]{1,0,2:T(8,128)(2,1)S(1)}, bf16[64,128,128]{1,0,2:T(8,128)(2,1)}, u32[]{:S(2)}, u32[]{:S(2)}) collective-permute-start(bf16[64,128,128]{1,0,2:T(8,128)(2,1)S(1)} %copy.58), channel_id=1, source_target_pairs={{32,0},{64,32},{96,64},{128,96},{160,128},{192,160},{224,192},{256... | collective-permute-start | bytes 6291464 | tf_op jit(solution)/shard_map/ppermute | solution.py:17
  119.5 47.5 %collective-permute-start.3 = (bf16[64,128,128]{1,0,2:T(8,128)(2,1)}, bf16[64,128,128]{1,0,2:T(8,128)(2,1)}, u32[]{:S(2)}, u32[]{:S(2)}) collective-permute-start(bf16[64,128,128]{1,0,2:T(8,128)(2,1)} %collective-permute-done.2), channel_id=1, source_target_pairs={{0,1},{1,2},{2,3},{3,4},{4,5},{5,6},{6,7},{7,8},{8,9},{9,10},{10,1... | collective-permute-start | bytes 6291464 | tf_op jit(solution)/shard_map/ppermute | solution.py:14
  124.9 47.6 %collective-permute-start.5 = (bf16[64,128,128]{1,0,2:T(8,128)(2,1)}, bf16[64,128,128]{1,0,2:T(8,128)(2,1)}, u32[]{:S(2)}, u32[]{:S(2)}) collective-permute-start(bf16[64,128,128]{1,0,2:T(8,128)(2,1)} %collective-permute-done.4), channel_id=1, source_target_pairs={{1,0},{2,1},{3,2},{4,3},{5,4},{6,5},{7,6},{8,7},{9,8},{10,9},{11,1... | collective-permute-start | bytes 6291464 | tf_op jit(solution)/shard_map/ppermute | solution.py:17
  189.8 9.8 %copy-start.5 = (f32[64]{0:T(128)S(1)}, f32[64]{0:T(128)}, u32[]{:S(2)}) copy-start(f32[64]{0:T(128)} %param.20) | copy-start | bytes 772
  204.8 3.4 copy-start.1
  204.8 3.4 copy-start.6
  204.8 3.4 copy-start.7
  204.8 3.4 copy-start.8
  204.8 3.4 copy-start.10
  278.2 184.0 %reduce-scatter.5.cloned.1.call-start = ((), (), s32[]{:S(2)}) async-start(), calls=%async_computation.4 | async-start | bytes 278528 | tf_op jit(solution)/shard_map/reduce_scatter | solution.py:129
Sparse Core Ops, SparseCore 0:
  278.3 91.4 reduce-scatter.2
  374.4 87.6 reduce-scatter.4
where the time goes:
time: 472 us; the launch traced here: 470 us
  waiting for transfers between devices  249 us (53%)
  local copies, waits for them, and re-layouts  64.1 us (14%)
  matrix products  63.5 us (13%)
  blocking collectives  35.8 us (8%)
  other arithmetic  21.6 us (5%)
  starting transfers between devices  18.6 us (4%)
  between operations  14.4 us (3%)
    reduce_scatter x1, waiting for transfers between devices, on_device(): lax.psum_scatter(squares, 'band', scatter_dimension=1, tiled=True)  92.3 us
    reduce_scatter x1, waiting for transfers between devices, on_device(): lax.psum_scatter(sums, 'band', scatter_dimension=1, tiled=True)  89.1 us
    ppermute x3, waiting for transfers between devices, padded_2(): lax.ppermute(lax.slice_in_dim(block, block.shape[dim] - width, None, axis...  64.3 us
    all_to_all x1, blocking collectives, on_device(): lax.all_to_all(spectral, 'band', split_axis=2, concat_axis=1, tiled=True)  35.8 us
    dot_general x4, matrix products, per_block(): jnp.einsum('et,cft->efc', member, block_out, precision=lax.Precision.HIGH...  19.6 us
    dot_general x4, matrix products, per_block(): jnp.einsum('et,cft->efc', member, block_out * block_out, precision=lax.Pr...  19.6 us
    unnamed x30, local copies, waits for them, and re-layouts  17.5 us
    dot_general x4, matrix products, per_block(): jnp.einsum('hc,hn->cn', w_down, hidden, preferred_element_type=jnp.float32)  12.4 us
  transfers between devices with their start and end apart: 8, of which 6 were waited for; matrix products, arithmetic and copies ran while one was open for 2% of the time, Pallas kernels for 0%

commit v1 on v0

--- a/solution.py
+++ b/solution.py
@@ -73,7 +73,10 @@
     all_bins = local_bins * bands
     padded = padded_2(spectrum, (("band", 1),), 2, False)
     spectral = bin_filter(padded, w_freq, b_freq, local_bins)
-    swapped = lax.all_to_all(spectral, "band", split_axis=2, concat_axis=1, tiled=True)
+    swapped = jnp.concatenate(
+        lax.all_to_all(jnp.stack(jnp.split(spectral, lax.axis_size("band"), axis=2)), "band", 0, 0),
+        axis=1,
+    )
     beside_all = padded_2(swapped, (("band", 2),), piece, True)
     outer_parts = jnp.concatenate([beside_all[:, :, 2 * piece :], beside_all[:, :, :piece]], axis=2)
     outer = padded_2(outer_parts, (("tm", 2),), piece, False)

time: 472 us -> 448 us (0.949)
  local copies, waits for them, and re-layouts: 64.1 us -> 40.5 us
    unnamed x30 -> x43, local copies, waits for them, and re-layouts: 17.5 us -> 4.51 us
    all_to_all x2 -> x0, local copies, waits for them, and re-layouts: 10.2 us -> none  [on_device(): lax.all_to_all(spectral, 'band', split_axis=2, concat_axis=1, tiled=True)]
where the time goes in v1:
time: 448 us; the launch traced here: 447 us
  waiting for transfers between devices  249 us (56%)
  matrix products  63.5 us (14%)
  local copies, waits for them, and re-layouts  40.5 us (9%)
  blocking collectives  35.8 us (8%)
  other arithmetic  21.6 us (5%)
  starting transfers between devices  18.6 us (4%)
  between operations  14.4 us (3%)
    reduce_scatter x1, waiting for transfers between devices, on_device(): lax.psum_scatter(squares, 'band', scatter_dimension=1, tiled=True)  92.3 us
    reduce_scatter x1, waiting for transfers between devices, on_device(): lax.psum_scatter(sums, 'band', scatter_dimension=1, tiled=True)  89.1 us
    ppermute x3, waiting for transfers between devices, padded_2(): lax.ppermute(lax.slice_in_dim(block, block.shape[dim] - width, None, axis...  64.1 us
    all_to_all x1, blocking collectives, on_device(): lax.all_to_all(jnp.stack(jnp.split(spectral, lax.axis_size('band'), axis=...  35.8 us
    dot_general x4, matrix products, per_block(): jnp.einsum('et,cft->efc', member, block_out, precision=lax.Precision.HIGH...  19.6 us
    dot_general x4, matrix products, per_block(): jnp.einsum('et,cft->efc', member, block_out * block_out, precision=lax.Pr...  19.6 us
    dot_general x4, matrix products, per_block(): jnp.einsum('hc,hn->cn', w_down, hidden, preferred_element_type=jnp.float32)  12.4 us
    ppermute x3, starting transfers between devices, padded_2(): lax.ppermute(lax.slice_in_dim(block, block.shape[dim] - width, None, axis...  10 us
  transfers between devices with their start and end apart: 8, of which 6 were waited for; matrix products, arithmetic and copies ran while one was open for 2% of the time, Pallas kernels for 0%

profile of v1, /device:TPU:2, one launch (start us, length us, event | category | flops | bytes accessed | tf_op | source)
XLA Modules:
  0.0 446.7 jit_solution(14770787725092758281)
XLA Ops:
  7.2 3.3 fusion.77
  10.7 1.9 collective-permute-start
  12.8 3.6 collective-permute-start.1
  16.6 2.8 fusion.70
  19.4 1.8 collective-permute-done
  21.2 1.2 constant_dynamic-update-slice_fusion
  22.5 0.7 fusion.50
  23.2 0.7 fusion.52
  23.9 0.7 fusion.48
  24.6 2.6 fusion.43
  28.1 35.8 %all_to_all.5 = bf16[16,64,8,128]{3,1,2,0:T(8,128)(2,1)} all-to-all(bf16[16,64,8,128]{3,1,2,0:T(8,128)(2,1)S(1)} %fusion.54), channel_id=1, replica_groups=mesh['band'=16,'tm'=32] {'band'}, dimensions={0} | all-to-all | bytes 4194304 | tf_op jit(solution)/shard_map/all_to_all | solution.py:77
  63.9 3.9 copy.20
  67.8 2.9 collective-permute-start.2
  70.7 3.4 collective-permute-start.4
  74.1 21.9 %collective-permute-done.2 = bf16[64,128,128]{1,0,2:T(8,128)(2,1)} collective-permute-done((bf16[64,128,128]{1,0,2:T(8,128)(2,1)S(1)}, bf16[64,128,128]{1,0,2:T(8,128)(2,1)}, u32[]{:S(2)}, u32[]{:S(2)}) %collective-permute-start.2) | collective-permute-done | bytes 2097184 | tf_op jit(solution)/shard_map/ppermute | solution.py:14
  96.0 5.2 %collective-permute-start.3 = (bf16[64,128,128]{1,0,2:T(8,128)(2,1)}, bf16[64,128,128]{1,0,2:T(8,128)(2,1)}, u32[]{:S(2)}, u32[]{:S(2)}) collective-permute-start(bf16[64,128,128]{1,0,2:T(8,128)(2,1)} %collective-permute-done.2), channel_id=1, source_target_pairs={{0,1},{1,2},{2,3},{3,4},{4,5},{5,6},{6,7},{7,8},{8,9},{9,10},{10,1... | collective-permute-start | bytes 6291464 | tf_op jit(solution)/shard_map/ppermute | solution.py:14
  101.2 1.5 collective-permute-start.5
  102.9 40.4 %collective-permute-done.3 = bf16[64,128,128]{1,0,2:T(8,128)(2,1)} collective-permute-done((bf16[64,128,128]{1,0,2:T(8,128)(2,1)}, bf16[64,128,128]{1,0,2:T(8,128)(2,1)}, u32[]{:S(2)}, u32[]{:S(2)}) %collective-permute-start.3) | collective-permute-done | bytes 2097184 | tf_op jit(solution)/shard_map/ppermute | solution.py:14
  143.4 1.8 broadcast_select_fusion.1
  145.2 3.6 collective-permute-done.5
  148.8 1.8 broadcast_select_fusion
  150.6 5.7 %pad_maximum_fusion = bf16[64,128,384]{1,0,2:T(8,128)(2,1)} fusion(bf16[64,128,128]{1,0,2:T(8,128)(2,1)S(1)} %broadcast_select_fusion, bf16[64,128,128]{1,0,2:T(8,128)(2,1)S(1)} %copy.20, bf16[64,128,128]{1,0,2:T(8,128)(2,1)S(1)} %broadcast_select_fusion.1), kind=kLoop, calls=%fused_computation.47 | loop fusion | flops 6291456 | bytes 12582912 | tf_op jit(solution)/shard_map/concatenate | solution.py:88
  156.3 9.8 %gather_fusion = bf16[64,128,128]{1,0,2:T(8,128)(2,1)} fusion(bf16[64,128,384]{1,0,2:T(8,128)(2,1)} %pad_maximum_fusion, s32[64]{0:T(128)S(1)} %get-tuple-element.153), kind=kCustom, calls=%fused_computation | custom fusion | bytes 4195072 | tf_op jit(solution)/shard_map/vmap()/gather | solution.py:25
  166.1 9.8 %gather_fusion.1 = bf16[64,128,128]{1,0,2:T(8,128)(2,1)} fusion(bf16[64,128,384]{1,0,2:T(8,128)(2,1)} %pad_maximum_fusion, s32[64]{0:T(128)S(1)} %get-tuple-element.154), kind=kCustom, calls=%fused_computation.1 | custom fusion | bytes 4195072 | tf_op jit(solution)/shard_map/vmap()/gather | solution.py:27
  175.9 5.2 %add_convert_fusion = bf16[64,128,128]{1,0,2:T(8,128)(2,1)} fusion(bf16[64,128,128]{1,0,2:T(8,128)(2,1)} %gather_fusion.1, bf16[64,128,128]{1,0,2:T(8,128)(2,1)S(1)} %copy.20, bf16[64,128,128]{1,0,2:T(8,128)(2,1)} %gather_fusion, f32[64]{0:T(128)S(1)} %copy-done.5, f32[64]{0:T(128)S(1)} %get-tuple-element.149, f32[64]{0:T(128)S(1)} %get-tuple-element.150, ...), kind=kLoop, calls=%fused_computation.57 | loop fusion | flops 10485760 | bytes 8389632 | tf_op jit(solution)/shard_map/convert_element_type | solution.py:30
  181.1 3.4 copy.24
  184.5 67.5 %while.13 = (s32[]{:T(128)}, f32[4,8,32,64]{2,1,3,0:T(8,128)}, f32[4,8,32,64]{2,1,3,0:T(8,128)}, s32[4]{0:T(128)S(1)}, bf16[128,128]{1,0:T(8,128)(2,1)}, /*index...) while((s32[]{:T(128)}, f32[4,8,32,64]{2,1,3,0:T(8,128)}, ...), condition=%wide.region_4.5_spmd.clone, body=%wide.region_1.4_spmd.clone.sunk | while | flops 399519744 | bytes 14905191 | solution.py:127
  184.8 0.6 dynamic_slice.25
  186.0 1.1 fusion.102
  187.3 1.0 multiply_convert_fusion.2
  188.3 3.1 fusion.103
  191.4 0.2 copy.43
  191.6 0.2 bitcast_add_fusion.2
  191.8 4.9 %fusion.105 = f32[4,8,32,64]{2,1,3,0:T(8,128)} fusion(f32[4,8,32,64]{2,1,3,0:T(8,128)} %get-tuple-element.264, s32[]{:T(128)} %get-tuple-element.262, f32[64,32,128]{2,1,0:T(8,128)S(1)} %bitcast_add_fusion.2, s32[128]{0:T(128)S(1)} %get-tuple-element.293, s32[8]{0:T(128)S(1)} %get-tuple-element.292, s32[8]{0:T(128)S(1)} %get-tuple-element.291), kind=kOutput, calls=%fused_computation.18.clone.1 | convolution fusion | flops 25432064 | bytes 1311808 | tf_op jit(solution)/shard_map/while/body/eval_jaxpr/et,cft->efc/dot_general | solution.py:122
  196.7 4.9 %fusion.104 = f32[4,8,32,64]{2,1,3,0:T(8,128)} fusion(f32[4,8,32,64]{2,1,3,0:T(8,128)} %get-tuple-element.263, s32[]{:T(128)} %get-tuple-element.262, f32[64,32,128]{2,1,0:T(8,128)S(1)} %bitcast_add_fusion.2, s32[128]{0:T(128)S(1)} %get-tuple-element.293, s32[8]{0:T(128)S(1)} %get-tuple-element.292, s32[8]{0:T(128)S(1)} %get-tuple-element.291), kind=kOutput, calls=%fused_computation.20.clone.1 | convolution fusion | flops 25169920 | bytes 1311808 | tf_op jit(solution)/shard_map/while/body/eval_jaxpr/et,cft->efc/dot_general | solution.py:121
  201.6 0.6 dynamic_slice.25
  202.9 1.1 fusion.102
  204.2 1.0 multiply_convert_fusion.2
  205.1 3.1 fusion.103
  208.2 0.2 copy.43
  208.6 4.9 %fusion.105 = f32[4,8,32,64]{2,1,3,0:T(8,128)} fusion(f32[4,8,32,64]{2,1,3,0:T(8,128)} %get-tuple-element.264, s32[]{:T(128)} %get-tuple-element.262, f32[64,32,128]{2,1,0:T(8,128)S(1)} %bitcast_add_fusion.2, s32[128]{0:T(128)S(1)} %get-tuple-element.293, s32[8]{0:T(128)S(1)} %get-tuple-element.292, s32[8]{0:T(128)S(1)} %get-tuple-element.291), kind=kOutput, calls=%fused_computation.18.clone.1 | convolution fusion | flops 25432064 | bytes 1311808 | tf_op jit(solution)/shard_map/while/body/eval_jaxpr/et,cft->efc/dot_general | solution.py:122
  213.5 4.9 %fusion.104 = f32[4,8,32,64]{2,1,3,0:T(8,128)} fusion(f32[4,8,32,64]{2,1,3,0:T(8,128)} %get-tuple-element.263, s32[]{:T(128)} %get-tuple-element.262, f32[64,32,128]{2,1,0:T(8,128)S(1)} %bitcast_add_fusion.2, s32[128]{0:T(128)S(1)} %get-tuple-element.293, s32[8]{0:T(128)S(1)} %get-tuple-element.292, s32[8]{0:T(128)S(1)} %get-tuple-element.291), kind=kOutput, calls=%fused_computation.20.clone.1 | convolution fusion | flops 25169920 | bytes 1311808 | tf_op jit(solution)/shard_map/while/body/eval_jaxpr/et,cft->efc/dot_general | solution.py:121
  218.4 0.6 dynamic_slice.25
  219.7 1.1 fusion.102
  221.0 1.0 multiply_convert_fusion.2
  221.9 3.1 fusion.103
  225.1 0.2 copy.43
  225.3 0.2 bitcast_add_fusion.2
  225.5 4.9 %fusion.105 = f32[4,8,32,64]{2,1,3,0:T(8,128)} fusion(f32[4,8,32,64]{2,1,3,0:T(8,128)} %get-tuple-element.264, s32[]{:T(128)} %get-tuple-element.262, f32[64,32,128]{2,1,0:T(8,128)S(1)} %bitcast_add_fusion.2, s32[128]{0:T(128)S(1)} %get-tuple-element.293, s32[8]{0:T(128)S(1)} %get-tuple-element.292, s32[8]{0:T(128)S(1)} %get-tuple-element.291), kind=kOutput, calls=%fused_computation.18.clone.1 | convolution fusion | flops 25432064 | bytes 1311808 | tf_op jit(solution)/shard_map/while/body/eval_jaxpr/et,cft->efc/dot_general | solution.py:122
  230.4 4.9 %fusion.104 = f32[4,8,32,64]{2,1,3,0:T(8,128)} fusion(f32[4,8,32,64]{2,1,3,0:T(8,128)} %get-tuple-element.263, s32[]{:T(128)} %get-tuple-element.262, f32[64,32,128]{2,1,0:T(8,128)S(1)} %bitcast_add_fusion.2, s32[128]{0:T(128)S(1)} %get-tuple-element.293, s32[8]{0:T(128)S(1)} %get-tuple-element.292, s32[8]{0:T(128)S(1)} %get-tuple-element.291), kind=kOutput, calls=%fused_computation.20.clone.1 | convolution fusion | flops 25169920 | bytes 1311808 | tf_op jit(solution)/shard_map/while/body/eval_jaxpr/et,cft->efc/dot_general | solution.py:121
  235.2 0.6 dynamic_slice.25
  236.5 1.1 fusion.102
  237.8 1.0 multiply_convert_fusion.2
  238.8 3.1 fusion.103
  241.9 0.2 copy.43
  242.3 4.9 %fusion.105 = f32[4,8,32,64]{2,1,3,0:T(8,128)} fusion(f32[4,8,32,64]{2,1,3,0:T(8,128)} %get-tuple-element.264, s32[]{:T(128)} %get-tuple-element.262, f32[64,32,128]{2,1,0:T(8,128)S(1)} %bitcast_add_fusion.2, s32[128]{0:T(128)S(1)} %get-tuple-element.293, s32[8]{0:T(128)S(1)} %get-tuple-element.292, s32[8]{0:T(128)S(1)} %get-tuple-element.291), kind=kOutput, calls=%fused_computation.18.clone.1 | convolution fusion | flops 25432064 | bytes 1311808 | tf_op jit(solution)/shard_map/while/body/eval_jaxpr/et,cft->efc/dot_general | solution.py:122
  247.2 4.9 %fusion.104 = f32[4,8,32,64]{2,1,3,0:T(8,128)} fusion(f32[4,8,32,64]{2,1,3,0:T(8,128)} %get-tuple-element.263, s32[]{:T(128)} %get-tuple-element.262, f32[64,32,128]{2,1,0:T(8,128)S(1)} %bitcast_add_fusion.2, s32[128]{0:T(128)S(1)} %get-tuple-element.293, s32[8]{0:T(128)S(1)} %get-tuple-element.292, s32[8]{0:T(128)S(1)} %get-tuple-element.291), kind=kOutput, calls=%fused_computation.20.clone.1 | convolution fusion | flops 25169920 | bytes 1311808 | tf_op jit(solution)/shard_map/while/body/eval_jaxpr/et,cft->efc/dot_general | solution.py:121
  252.0 1.5 copy.25
  253.6 0.9 reshape.138
  254.5 1.5 copy.26
  256.1 0.9 reshape.139
  257.0 89.1 %reduce-scatter.3.cloned.1.call-done = f32[8,512]{1,0:T(8,128)} async-done(((f32[8,8192]{1,0:T(8,128)}), f32[8,512]{1,0:T(8,128)}) %reduce-scatter.3.cloned.1.call-update) | async-done | bytes 16400 | tf_op jit(solution)/shard_map/reduce_scatter | solution.py:131
  346.1 92.3 %reduce-scatter.5.cloned.1.call-done = f32[8,512]{1,0:T(8,128)} async-done(((f32[8,8192]{1,0:T(8,128)}), f32[8,512]{1,0:T(8,128)}) %reduce-scatter.5.cloned.1.call-update) | async-done | bytes 16400 | tf_op jit(solution)/shard_map/reduce_scatter | solution.py:132
  438.4 1.4 broadcast_divide_fusion
  (76 shorter events, 2.8 us)
Async XLA Ops:
  7.2 9.4 %copy-start = (bf16[64,8,2048]{2,1,0:T(8,128)(2,1)S(1)}, bf16[64,8,2048]{2,1,0:T(8,128)(2,1)}, u32[]{:S(2)}) copy-start(bf16[64,8,2048]{2,1,0:T(8,128)(2,1)} %param.15) | copy-start | bytes 6291460
  7.2 9.4 %copy-start.2 = (bf16[5,64,8]{1,2,0:T(8,128)(2,1)S(1)}, bf16[5,64,8]{1,2,0:T(8,128)(2,1)}, u32[]{:S(2)}) copy-start(bf16[5,64,8]{1,2,0:T(8,128)(2,1)} %param.16) | copy-start | bytes 15364
  7.2 338.9 %reduce-scatter.3.cloned.1.call-start = ((), (), s32[]{:S(2)}) async-start(), calls=%async_computation.3 | async-start | bytes 278528 | tf_op jit(solution)/shard_map/reduce_scatter | solution.py:131
  10.7 10.5 %collective-permute-start = (bf16[64,2,2048]{2,0,1:T(8,128)(2,1)S(1)}, bf16[64,2,2048]{2,0,1:T(8,128)(2,1)S(1)}, u32[]{:S(2)}, u32[]{:S(2)}) collective-permute-start(bf16[64,2,2048]{2,0,1:T(8,128)(2,1)S(1)} %copy.39), channel_id=1, source_target_pairs={{0,32},{32,64},{64,96},{96,128},{128,160},{160,192},{192,224},{224... | collective-permute-start | bytes 1572872 | tf_op jit(solution)/shard_map/ppermute | solution.py:14
  12.8 11.1 %collective-permute-start.1 = (bf16[64,2,2048]{2,0,1:T(8,128)(2,1)S(1)}, bf16[64,2,2048]{2,0,1:T(8,128)(2,1)S(1)}, u32[]{:S(2)}, u32[]{:S(2)}) collective-permute-start(bf16[64,2,2048]{2,0,1:T(8,128)(2,1)S(1)} %copy.38), channel_id=1, source_target_pairs={{32,0},{64,32},{96,64},{128,96},{160,128},{192,160},{224,192},{256... | collective-permute-start | bytes 1572872 | tf_op jit(solution)/shard_map/ppermute | solution.py:17
  23.9 0.7 copy-start.4
  63.9 38.8 %copy-start.11 = (s32[1,8]{1,0:T(1,128)S(1)}, s32[1,8]{1,0:T(1,128)}, u32[]{:S(2)}) copy-start(s32[1,8]{1,0:T(1,128)} %param.27) | copy-start | bytes 100
  63.9 39.0 %copy-start.9 = (s32[64]{0:T(128)S(1)}, s32[64]{0:T(128)}, u32[]{:S(2)}) copy-start(s32[64]{0:T(128)} %param.18) | copy-start | bytes 772
  63.9 39.0 %copy-start.3 = (f32[3,64]{1,0:T(4,128)S(1)}, f32[3,64]{1,0:T(4,128)}, u32[]{:S(2)}) copy-start(f32[3,64]{1,0:T(4,128)} %param.19) | copy-start | bytes 2308
  67.8 28.2 %collective-permute-start.2 = (bf16[64,128,128]{1,0,2:T(8,128)(2,1)S(1)}, bf16[64,128,128]{1,0,2:T(8,128)(2,1)}, u32[]{:S(2)}, u32[]{:S(2)}) collective-permute-start(bf16[64,128,128]{1,0,2:T(8,128)(2,1)S(1)} %copy.20), channel_id=1, source_target_pairs={{0,32},{32,64},{64,96},{96,128},{128,160},{160,192},{192,224},{224... | collective-permute-start | bytes 6291464 | tf_op jit(solution)/shard_map/ppermute | solution.py:14
  70.7 30.4 %collective-permute-start.4 = (bf16[64,128,128]{1,0,2:T(8,128)(2,1)S(1)}, bf16[64,128,128]{1,0,2:T(8,128)(2,1)}, u32[]{:S(2)}, u32[]{:S(2)}) collective-permute-start(bf16[64,128,128]{1,0,2:T(8,128)(2,1)S(1)} %copy.20), channel_id=1, source_target_pairs={{32,0},{64,32},{96,64},{128,96},{160,128},{192,160},{224,192},{256... | collective-permute-start | bytes 6291464 | tf_op jit(solution)/shard_map/ppermute | solution.py:17
  96.0 47.3 %collective-permute-start.3 = (bf16[64,128,128]{1,0,2:T(8,128)(2,1)}, bf16[64,128,128]{1,0,2:T(8,128)(2,1)}, u32[]{:S(2)}, u32[]{:S(2)}) collective-permute-start(bf16[64,128,128]{1,0,2:T(8,128)(2,1)} %collective-permute-done.2), channel_id=1, source_target_pairs={{0,1},{1,2},{2,3},{3,4},{4,5},{5,6},{6,7},{7,8},{8,9},{9,10},{10,1... | collective-permute-start | bytes 6291464 | tf_op jit(solution)/shard_map/ppermute | solution.py:14
  101.2 47.6 %collective-permute-start.5 = (bf16[64,128,128]{1,0,2:T(8,128)(2,1)}, bf16[64,128,128]{1,0,2:T(8,128)(2,1)}, u32[]{:S(2)}, u32[]{:S(2)}) collective-permute-start(bf16[64,128,128]{1,0,2:T(8,128)(2,1)} %collective-permute-done.4), channel_id=1, source_target_pairs={{1,0},{2,1},{3,2},{4,3},{5,4},{6,5},{7,6},{8,7},{9,8},{10,9},{11,1... | collective-permute-start | bytes 6291464 | tf_op jit(solution)/shard_map/ppermute | solution.py:17
  166.1 9.8 %copy-start.5 = (f32[64]{0:T(128)S(1)}, f32[64]{0:T(128)}, u32[]{:S(2)}) copy-start(f32[64]{0:T(128)} %param.20) | copy-start | bytes 772
  181.1 3.4 copy-start.1
  181.1 3.4 copy-start.6
  181.1 3.4 copy-start.7
  181.1 3.4 copy-start.8
  181.1 3.4 copy-start.10
  254.5 183.9 %reduce-scatter.5.cloned.1.call-start = ((), (), s32[]{:S(2)}) async-start(), calls=%async_computation.4 | async-start | bytes 278528 | tf_op jit(solution)/shard_map/reduce_scatter | solution.py:132
Sparse Core Ops, SparseCore 0:
  254.6 91.4 reduce-scatter.2
  350.7 87.6 reduce-scatter.4
